TPU v7x, 32 devices: a whole 2x2x4 slice. The times are simulated.
32 devices in a mesh: dp: 4 (over x, core), seq: 4 (over z), tensor: 2 (over y).
Axes of the slice: x: 2, y: 2, z: 4, core: 2. Of those that a mesh axis runs over, the one named last changes fastest.
Arguments:
- queries: bfloat16 [4, 2048, 1024], P('dp', 'seq', 'tensor'), may hold values from -6 to 6
- key_vectors: bfloat16 [4, 2048, 1024], P('dp', 'seq', 'tensor'), may hold values from -6 to 6
- value_vectors: bfloat16 [4, 2048, 1024], P('dp', 'seq', 'tensor'), may hold values from -6 to 6
- log_decay: float32 [4, 8, 2048], P('dp', 'tensor'), may hold values from -0.75 to 0
- w_out: bfloat16 [1024, 3072], P('tensor'), may hold values from -0.1875 to 0.1875
- grad_out: bfloat16 [4, 2048, 3072], P('dp', 'seq', 'tensor'), may hold values from -6 to 6
Outputs:
- grad_queries: bfloat16 [4, 2048, 1024], P('dp', 'seq', 'tensor')
- grad_keys: bfloat16 [4, 2048, 1024], P('dp', 'seq', 'tensor')
- grad_values: bfloat16 [4, 2048, 1024], P('dp', 'seq', 'tensor')
- grad_w_t: float32 [3072, 1024], P(('dp', 'seq'), 'tensor')
All inputs are finite; a program needn't handle non-finite values.
Results may differ from a plain program's by a relative error of at most 0.015.
Values may be sent and summed in bfloat16 or wider, within the bound.
No kernel may reach another device: no remote copies, remote signals or barrier semaphores. Data moves between devices by JAX's collectives and lax.ppermute only.
A program may use at most 64 MiB of HBM per device.

v0:
```python
import math
import jax
import jax.numpy as jnp
from jax import lax
from jax.sharding import PartitionSpec as P

D = 3072
highest_precision = lax.Precision.HIGHEST


def decay_matrix(cumulative):
    size_now = cumulative.shape[-1]
    later_pos = lax.broadcasted_iota(jnp.int32, (size_now, size_now), 0)
    earlier_pos = lax.broadcasted_iota(jnp.int32, (size_now, size_now), 1)
    lower = later_pos >= earlier_pos
    spread = cumulative[..., :, None] - cumulative[..., None, :]
    return jnp.where(lower, jnp.exp(jnp.where(lower, spread, 0.0)), 0.0)


def local(queries, key_vectors, value_vectors, log_decay, w_out, grad_out):
    micro_count, row_count, feature_width = queries.shape
    head_count = log_decay.shape[1]
    head_dim = feature_width // head_count
    flat_size = head_dim * head_dim
    seq_count = lax.axis_size("seq")
    seq_index = lax.axis_index("seq")
    inverse = 1.0 / head_dim
    grad_scale = 1.0 / math.sqrt(micro_count * lax.axis_size("dp") * row_count * seq_count)
    block_totals = jnp.sum(log_decay.reshape(micro_count, head_count, seq_count, row_count), axis=3)
    block_ends = jnp.cumsum(block_totals, axis=2)
    block_starts = block_ends - block_totals
    start_here = lax.dynamic_index_in_dim(block_starts, seq_index, axis=2, keepdims=False)
    end_here = lax.dynamic_index_in_dim(block_ends, seq_index, axis=2, keepdims=False)
    local_decay = lax.dynamic_slice_in_dim(log_decay, seq_index * row_count, row_count, axis=2)
    cumulative = jnp.cumsum(local_decay, axis=2)
    own_total = cumulative[:, :, -1]
    decay_mask = decay_matrix(cumulative)
    from_start = jnp.transpose(jnp.exp(cumulative), (0, 2, 1))[..., None]
    to_end = jnp.transpose(jnp.exp(own_total[:, :, None] - cumulative), (0, 2, 1))[..., None]
    query_heads = queries.reshape(micro_count, row_count, head_count, head_dim)
    key_heads = key_vectors.reshape(micro_count, row_count, head_count, head_dim)
    value_heads = value_vectors.reshape(micro_count, row_count, head_count, head_dim)
    query_float = query_heads.astype(jnp.float32)
    key_float = key_heads.astype(jnp.float32)
    value_float = value_heads.astype(jnp.float32)
    empty_states = jnp.zeros((micro_count, head_count, flat_size), jnp.float32)
    scores = jnp.einsum(
        "mthd,mshd->mhts", query_heads, key_heads, preferred_element_type=jnp.float32
    )
    weights = (scores * decay_mask * inverse).astype(jnp.bfloat16)
    local_state = jnp.einsum(
        "mshd,mshe->mhde", key_float * to_end, value_float, precision=highest_precision
    )
    shard_piece = lax.all_gather(
        local_state.reshape(1, micro_count, head_count, flat_size).astype(jnp.bfloat16),
        "seq",
        axis=0,
        tiled=True,
    ).astype(jnp.float32)
    piece_rows = shard_piece.shape[0]
    position = jnp.arange(piece_rows, dtype=jnp.int32)
    factor = jnp.where(
        position[None, None, :] < seq_index,
        jnp.exp(jnp.minimum(start_here[:, :, None] - block_ends, 0.0)),
        0.0,
    )
    incoming = empty_states + jnp.einsum(
        "nmhx,mhn->mhx", shard_piece, factor, precision=highest_precision
    )
    carried = incoming.reshape(micro_count, head_count, head_dim, head_dim)
    within_block = jnp.einsum(
        "mhts,mshd->mthd", weights, value_heads, preferred_element_type=jnp.float32
    )
    from_carried = jnp.einsum(
        "mthd,mhde->mthe", query_float * from_start, carried, precision=highest_precision
    )
    attn_out = (
        (within_block + from_carried * inverse)
        .astype(jnp.bfloat16)
        .reshape(micro_count, row_count, feature_width)
    )
    shard_piece = lax.all_gather(grad_out, "tensor", axis=2, tiled=True)
    attn_running = jnp.einsum("mcd,fd->mcf", shard_piece, w_out, preferred_element_type=jnp.float32)
    column_block = jnp.einsum(
        "mcd,mcf->df", shard_piece, attn_out, preferred_element_type=jnp.float32
    )
    grad_attn = attn_running.astype(jnp.bfloat16)
    rounded = lax.optimization_barrier((column_block * grad_scale).astype(jnp.bfloat16)).astype(
        jnp.float32
    )
    reordered = jnp.transpose(
        rounded.reshape(
            lax.axis_size("dp"), seq_count, D // (lax.axis_size("dp") * seq_count), feature_width
        ),
        (1, 0, 2, 3),
    ).reshape(D, feature_width)
    reduced = lax.psum_scatter(
        reordered.astype(jnp.bfloat16), "seq", scatter_dimension=0, tiled=True
    )
    grad_w_t = lax.psum_scatter(reduced, "dp", scatter_dimension=0, tiled=True).astype(jnp.float32)
    grad_heads = grad_attn.reshape(micro_count, row_count, head_count, head_dim)
    grad_float = grad_heads.astype(jnp.float32)
    grad_scores = jnp.einsum(
        "mthd,mshd->mhts", grad_heads, value_heads, preferred_element_type=jnp.float32
    )
    grad_weights = (grad_scores * decay_mask * inverse).astype(jnp.bfloat16)
    local_back = (
        jnp.einsum(
            "mthd,mthe->mhde", query_float * from_start, grad_float, precision=highest_precision
        )
        * inverse
    )
    shard_piece = lax.all_gather(
        local_back.reshape(1, micro_count, head_count, flat_size).astype(jnp.bfloat16),
        "seq",
        axis=0,
        tiled=True,
    ).astype(jnp.float32)
    piece_rows = shard_piece.shape[0]
    position = jnp.arange(piece_rows, dtype=jnp.int32)
    factor = jnp.where(
        position[None, None, :] > seq_index,
        jnp.exp(jnp.minimum(block_starts - end_here[:, :, None], 0.0)),
        0.0,
    )
    outgoing = empty_states + jnp.einsum(
        "nmhx,mhn->mhx", shard_piece, factor, precision=highest_precision
    )
    back_state = outgoing.reshape(micro_count, head_count, head_dim, head_dim)
    grad_queries = (
        jnp.einsum("mhts,mshd->mthd", grad_weights, key_heads, preferred_element_type=jnp.float32)
        + jnp.einsum(
            "mthe,mhde->mthd", grad_float * from_start, carried, precision=highest_precision
        )
        * inverse
    )
    grad_keys = jnp.einsum(
        "mhts,mthd->mshd", grad_weights, query_heads, preferred_element_type=jnp.float32
    ) + jnp.einsum("mshe,mhde->mshd", value_float * to_end, back_state, precision=highest_precision)
    grad_values = jnp.einsum(
        "mhts,mthd->mshd", weights, grad_heads, preferred_element_type=jnp.float32
    ) + jnp.einsum("mshd,mhde->mshe", key_float * to_end, back_state, precision=highest_precision)
    out_shape = (micro_count, row_count, feature_width)
    return (
        grad_queries.astype(jnp.bfloat16).reshape(out_shape),
        grad_keys.astype(jnp.bfloat16).reshape(out_shape),
        grad_values.astype(jnp.bfloat16).reshape(out_shape),
        grad_w_t,
    )


def solution(mesh):
    in_specs = (
        P("dp", "seq", "tensor"),
        P("dp", "seq", "tensor"),
        P("dp", "seq", "tensor"),
        P("dp", "tensor", None),
        P("tensor", None),
        P("dp", "seq", "tensor"),
    )
    out_specs = (
        P("dp", "seq", "tensor"),
        P("dp", "seq", "tensor"),
        P("dp", "seq", "tensor"),
        P(("dp", "seq"), "tensor"),
    )
    return jax.shard_map(local, mesh=mesh, in_specs=in_specs, out_specs=out_specs, check_vma=False)
```

profile of v0, /device:TPU:0, one launch (start us, length us, event | category | flops | bytes accessed | tf_op | source)
XLA Modules:
  0.0 169.6 jit_solution(3306231275859728322)
XLA Ops:
  12.3 2.0 %reshape.419 = bf16[512,4,128]{2,1,0:T(4,128)(2,1)} reshape(bf16[1,512,512]{2,1,0:T(8,128)(2,1)} %param.8) | data formatting | bytes 1048576 | tf_op jit(solution)/shard_map/reshape.6
  14.2 2.0 %reshape.425 = bf16[512,4,128]{2,1,0:T(4,128)(2,1)} reshape(bf16[1,512,512]{2,1,0:T(8,128)(2,1)} %param.7) | data formatting | bytes 1048576 | tf_op jit(solution)/shard_map/reshape.13
  21.1 2.6 %convolution_convert_fusion = bf16[4,128,128]{2,1,0:T(8,128)(2,1)S(1)} fusion(f32[512,4]{0,1:T(4,128)S(1)} %copy.96, bf16[512,4,128]{2,1,0:T(4,128)(2,1)} %reshape.425, bf16[512,4,128]{2,1,0:T(4,128)(2,1)} %reshape.419), kind=kOutput, calls=%fused_computation.24 | convolution fusion | flops 403243008 | bytes 1187840 | tf_op jit(solution)/shard_map/mshd,mshe->mhde/dot_general | solution.py:51
  24.0 17.4 %all_gather.10 = bf16[4,1,4,16384]{3,2,1,0:T(4,128)(2,1)S(1)} all-gather(bf16[1,1,4,16384]{3,2,1,0:T(4,128)(2,1)S(1)} %convert_element_type.128), channel_id=1, replica_groups=mesh['dp'=4,'seq'=4,'tensor'=2] {'seq'}, dimensions={0}, use_global_device_ids=true | all-gather | bytes 655360 | tf_op jit(solution)/shard_map/all_gather | solution.py:54
  43.0 2.0 %reshape.432 = bf16[512,4,128]{2,1,0:T(4,128)(2,1)} reshape(bf16[1,512,512]{2,1,0:T(8,128)(2,1)} %param.6) | data formatting | bytes 1048576 | tf_op jit(solution)/shard_map/reshape.51
  45.1 2.8 %multiply_convert_fusion.1 = bf16[4,512,512]{2,1,0:T(8,128)(2,1)S(1)} fusion(f32[4,512]{1,0:T(4,128)S(1)} %bitcast_add_fusion.1, pred[512,512]{1,0:T(8,128)(4,1)S(1)} %iota_compare_fusion, bf16[512,4,128]{2,1,0:T(4,128)(2,1)} %reshape.432, bf16[512,4,128]{2,1,0:T(4,128)(2,1)} %reshape.425), kind=kOutput, calls=%fused_computation.1 | convolution fusion | flops 274726912 | bytes 3416064 | tf_op jit(solution)/shard_map/mthd,mshd->mhts/dot_general | solution.py:47
  50.3 2.2 %fusion.12 = bf16[4,128,512]{2,1,0:T(8,128)(2,1)} fusion(f32[4,128,512]{2,1,0:T(8,128)S(1)} %convolution_bitcast_fusion.1, f32[512,4]{0,1:T(4,128)S(1)} %copy.100, bf16[512,4,128]{2,1,0:T(4,128)(2,1)S(1)} %copy-done.8, f32[1,4,128,128]{3,1,2,0:T(4,128)S(1)} %bitcast.122), kind=kOutput, calls=%fused_computation.21 | convolution fusion | flops 403963904 | bytes 2367488 | tf_op jit(solution)/shard_map/mthd,mhde->mthe/dot_general | solution.py:74
  52.5 4.7 %all-gather.2.cloned.1.call-done = bf16[1,512,3072]{2,1,0:T(8,128)(2,1)} async-done(((bf16[1,512,1536]{2,1,0:T(8,128)(2,1)}), bf16[1,512,3072]{2,1,0:T(8,128)(2,1)}) %all-gather.2.cloned.1.call-update) | async-done | bytes 3145744 | tf_op jit(solution)/shard_map/all_gather | solution.py:82
  57.2 5.6 %fusion = bf16[3072,512]{0,1:T(8,128)(2,1)} fusion(bf16[512,512]{0,1:T(8,128)(2,1)} %bitcast.136, bf16[1,512,3072]{2,1,0:T(8,128)(2,1)} %all-gather.2.cloned.1.call-done), kind=kOutput, calls=%fused_computation.4 | convolution fusion | flops 1613758464 | bytes 6815744 | tf_op jit(solution)/shard_map/mcd,mcf->df/dot_general | solution.py:84
  62.8 4.7 %copy.111 = bf16[3072,512]{1,0:T(8,128)(2,1)} copy(bf16[3072,512]{0,1:T(8,128)(2,1)} %fusion) | data formatting | bytes 6291456 | tf_op jit(solution)/shard_map/optimization_barrier | solution.py:88
  67.6 3.9 %copy.112 = bf16[4,4,192,512]{3,2,1,0:T(8,128)(2,1)} copy(bf16[4,4,192,512]{3,2,0,1:T(8,128)(2,1)} %bitcast.121) | data formatting | bytes 6291456 | tf_op jit(solution)/shard_map/convert_element_type | solution.py:98
  71.7 4.5 %fusion.6 = bf16[512,512]{0,1:T(8,128)(2,1)} fusion(bf16[512,3072]{1,0:T(8,128)(2,1)S(1)} %copy-done, bf16[1,512,3072]{2,1,0:T(8,128)(2,1)} %all-gather.2.cloned.1.call-done), kind=kOutput, calls=%fused_computation.17 | convolution fusion | flops 1610874880 | bytes 6815744 | tf_op jit(solution)/shard_map/mcd,fd->mcf/dot_general | solution.py:83
  76.2 2.0 %copy.99 = bf16[512,4,128]{2,0,1:T(8,128)(2,1)} copy(bf16[512,4,128]{0,2,1:T(8,128)(2,1)} %bitcast.126) | data formatting | bytes 1048576 | tf_op jit(solution)/shard_map/reshape.5
  78.2 3.0 %multiply_convert_fusion.2 = bf16[4,512,512]{2,1,0:T(8,128)(2,1)S(1)} fusion(bf16[512,4,128]{0,2,1:T(8,128)(2,1)} %bitcast.127, f32[4,512]{1,0:T(4,128)S(1)} %bitcast_add_fusion.1, pred[512,512]{1,0:T(8,128)(4,1)} %copy-done.10, bf16[512,4,128]{2,1,0:T(4,128)(2,1)} %reshape.419), kind=kOutput, calls=%fused_computation.2 | convolution fusion | flops 274726912 | bytes 3416064 | tf_op jit(solution)/shard_map/mthd,mshd->mhts/dot_general | solution.py:103
  83.6 2.1 %fusion.9 = bf16[4,128,512]{2,1,0:T(8,128)(2,1)} fusion(f32[4,128,512]{2,1,0:T(8,128)S(1)} %convolution_bitcast_fusion.2, bf16[512,4,128]{2,0,1:T(8,128)(2,1)S(1)} %copy-done.9, f32[512,4]{0,1:T(4,128)S(1)} %copy.100, f32[1,4,128,128]{3,1,2,0:T(4,128)S(1)} %bitcast.123), kind=kOutput, calls=%fused_computation.18 | convolution fusion | flops 403963904 | bytes 2367488 | tf_op jit(solution)/shard_map/mthe,mhde->mthd/dot_general | solution.py:132
  85.7 2.0 %copy.113 = bf16[1,512,512]{2,1,0:T(8,128)(2,1)} copy(bf16[1,512,512]{1,2,0:T(8,128)(2,1)} %bitcast.131) | data formatting | bytes 1048576
  87.8 2.5 %fusion.13 = bf16[4,128,128]{2,1,0:T(8,128)(2,1)S(1)} fusion(bf16[512,4,128]{0,2,1:T(8,128)(2,1)} %bitcast.128, f32[512,4]{0,1:T(4,128)S(1)} %copy.100, bf16[512,4,128]{2,1,0:T(4,128)(2,1)} %reshape.432), kind=kOutput, calls=%fused_computation.23 | convolution fusion | flops 403308544 | bytes 1187840 | tf_op jit(solution)/shard_map/mthd,mthe->mhde/dot_general | solution.py:108
  90.4 41.6 %reduce-scatter.3.cloned.1.call-done = bf16[768,512]{1,0:T(8,128)(2,1)} async-done(((bf16[3072,512]{1,0:T(8,128)(2,1)}), bf16[768,512]{1,0:T(8,128)(2,1)}) %reduce-scatter.3.cloned.1.call-update) | async-done | bytes 786448 | tf_op jit(solution)/shard_map/reduce_scatter | solution.py:97
  132.0 15.6 %all_gather.11 = bf16[4,1,4,16384]{3,2,1,0:T(4,128)(2,1)S(1)} all-gather(bf16[1,1,4,16384]{3,2,1,0:T(4,128)(2,1)S(1)} %convert_element_type.135), channel_id=1, replica_groups=mesh['dp'=4,'seq'=4,'tensor'=2] {'seq'}, dimensions={0}, use_global_device_ids=true | all-gather | bytes 655360 | tf_op jit(solution)/shard_map/all_gather | solution.py:113
  150.7 2.1 %fusion.10 = bf16[4,128,512]{2,1,0:T(8,128)(2,1)} fusion(f32[4,128,512]{2,1,0:T(8,128)S(1)} %convolution_bitcast_fusion, f32[512,4]{0,1:T(4,128)S(1)} %copy.96, bf16[512,4,128]{2,1,0:T(4,128)(2,1)S(1)} %copy-done.7, f32[1,4,128,128]{3,1,2,0:T(4,128)S(1)} %bitcast.124), kind=kOutput, calls=%fused_computation.19 | convolution fusion | flops 403701760 | bytes 2367488 | tf_op jit(solution)/shard_map/mshe,mhde->mshd/dot_general | solution.py:139
  152.8 2.0 %copy.114 = bf16[1,512,512]{2,1,0:T(8,128)(2,1)} copy(bf16[1,512,512]{1,2,0:T(8,128)(2,1)} %bitcast.132) | data formatting | bytes 1048576
  154.8 2.3 %fusion.55 = f32[4,128,512]{2,1,0:T(8,128)S(1)} fusion(bf16[512,4,128]{0,2,1:T(8,128)(2,1)} %bitcast.129, bf16[4,512,512]{2,1,0:T(8,128)(2,1)} %copy-done.1), kind=kOutput, calls=%fused_computation.86 | convolution fusion | flops 268435456 | bytes 3670016 | tf_op jit(solution)/shard_map/mhts,mthd->mshd/dot_general | solution.py:140
  157.1 2.2 %fusion.11 = bf16[4,128,512]{2,1,0:T(8,128)(2,1)} fusion(f32[4,128,512]{2,1,0:T(8,128)S(1)} %fusion.55, f32[512,4]{0,1:T(4,128)S(1)} %copy.96, bf16[512,4,128]{2,1,0:T(4,128)(2,1)S(1)} %copy-done.5, f32[1,4,128,128]{3,1,2,0:T(4,128)S(1)} %bitcast.125), kind=kOutput, calls=%fused_computation.20 | convolution fusion | flops 403701760 | bytes 2367488 | tf_op jit(solution)/shard_map/mshd,mhde->mshe/dot_general | solution.py:142
  159.3 2.0 %copy.115 = bf16[1,512,512]{2,1,0:T(8,128)(2,1)} copy(bf16[1,512,512]{1,2,0:T(8,128)(2,1)} %bitcast.130) | data formatting | bytes 1048576
  (63 shorter events, 21.7 us)
Async XLA Ops:
  7.2 64.5 %copy-start = (bf16[512,3072]{1,0:T(8,128)(2,1)S(1)}, bf16[512,3072]{1,0:T(8,128)(2,1)}, u32[]{:S(2)}) copy-start(bf16[512,3072]{1,0:T(8,128)(2,1)} %param.10) | copy-start | bytes 9437188
  7.2 50.1 %all-gather.2.cloned.1.call-start = ((), (), s32[]{:S(2)}) async-start(), calls=%async_computation.2 | async-start | bytes 4718592 | tf_op jit(solution)/shard_map/all_gather | solution.py:82
  7.9 124.1 %reduce-scatter.3.cloned.1.call-start = ((), (), s32[]{:S(2)}) async-start(), calls=%async_computation.3 | async-start | bytes 3932160 | tf_op jit(solution)/shard_map/reduce_scatter | solution.py:97
  45.1 2.8 %copy-start.10 = (pred[512,512]{1,0:T(8,128)(4,1)}, pred[512,512]{1,0:T(8,128)(4,1)S(1)}, u32[]{:S(2)}) copy-start(pred[512,512]{1,0:T(8,128)(4,1)S(1)} %iota_compare_fusion) | copy-start | bytes 786436
  45.1 4.1 %copy-start.6 = (bf16[512,4,128]{2,1,0:T(4,128)(2,1)S(1)}, bf16[512,4,128]{2,1,0:T(4,128)(2,1)}, u32[]{:S(2)}) copy-start(bf16[512,4,128]{2,1,0:T(4,128)(2,1)} %reshape.419) | copy-start | bytes 1572868
  47.9 1.3 copy-start.1
  49.2 1.0 copy-start.8
  71.4 89.9 %reduce-scatter.5.cloned.1.call-start = ((), (), s32[]{:S(2)}) async-start(), calls=%async_computation.4 | async-start | bytes 983040 | tf_op jit(solution)/shard_map/reduce_scatter | solution.py:100
  78.2 4.4 %copy-start.4 = (bf16[512,4,128]{2,1,0:T(4,128)(2,1)S(1)}, bf16[512,4,128]{2,1,0:T(4,128)(2,1)}, u32[]{:S(2)}) copy-start(bf16[512,4,128]{2,1,0:T(4,128)(2,1)} %reshape.425) | copy-start | bytes 1572868
  81.2 1.4 copy-start.2
  82.6 1.0 copy-start.9
  132.0 17.1 %copy-start.3 = (bf16[4,512,512]{2,1,0:T(8,128)(2,1)S(1)}, bf16[4,512,512]{2,1,0:T(8,128)(2,1)}, u32[]{:S(2)}) copy-start(bf16[4,512,512]{2,1,0:T(8,128)(2,1)} %copy-done.2) | copy-start | bytes 6291460
  132.0 18.7 %copy-start.7 = (bf16[512,4,128]{2,1,0:T(4,128)(2,1)S(1)}, bf16[512,4,128]{2,1,0:T(4,128)(2,1)}, u32[]{:S(2)}) copy-start(bf16[512,4,128]{2,1,0:T(4,128)(2,1)} %reshape.419) | copy-start | bytes 1572868
  154.8 2.3 %copy-start.5 = (bf16[512,4,128]{2,1,0:T(4,128)(2,1)S(1)}, bf16[512,4,128]{2,1,0:T(4,128)(2,1)}, u32[]{:S(2)}) copy-start(bf16[512,4,128]{2,1,0:T(4,128)(2,1)} %reshape.425) | copy-start | bytes 1572868
Sparse Core Ops, SparseCore 0:
  9.5 47.6 all-gather.1
  71.6 60.3 reduce-scatter.2
  134.5 23.1 reduce-scatter.4
where the time goes:
time: 171 us; the launch traced here: 170 us
  waiting for transfers between devices  47.1 us (28%)
  matrix products  37.6 us (22%)
  blocking collectives  33 us (19%)
  local copies, waits for them, and re-layouts  31.6 us (18%)
  between operations  14 us (8%)
  other arithmetic  6 us (4%)
    reduce_scatter x1, waiting for transfers between devices, local(): lax.psum_scatter(reordered.astype(jnp.bfloat16), 'seq', scatter_dimension...  41.6 us
    all_gather x1, blocking collectives, local(): lax.all_gather(local_state.reshape(1, micro_count, head_count, flat_size)...  17.4 us
    all_gather x1, blocking collectives, local(): lax.all_gather(local_back.reshape(1, micro_count, head_count, flat_size)....  15.6 us
    unnamed x25, local copies, waits for them, and re-layouts  9.27 us
    another operation x9, local copies, waits for them, and re-layouts  9.03 us
    dot_general x1, matrix products, local(): jnp.einsum('mcd,mcf->df', shard_piece, attn_out, preferred_element_type=j...  5.58 us
    all_gather x1, waiting for transfers between devices, local(): shard_piece = lax.all_gather(grad_out, 'tensor', axis=2, tiled=True)  4.74 us
    optimization_barrier x1, local copies, waits for them, and re-layouts, local(): lax.optimization_barrier((column_block * grad_scale).astype(jnp.bfloat16))  4.74 us
  transfers between devices with their start and end apart: 3, of which 2 were waited for; matrix products, arithmetic and copies ran while one was open for 33% of the time, Pallas kernels for 0%

commit v1 on v0

--- a/solution.py
+++ b/solution.py
@@ -6,6 +6,27 @@
 
 D = 3072
 highest_precision = lax.Precision.HIGHEST
+
+
+def joined_along(tiles, dim):
+    tiles = jnp.moveaxis(tiles, 0, dim)
+    shape = tiles.shape
+    return tiles.reshape(*shape[:dim], shape[dim] * shape[dim + 1], *shape[dim + 2 :])
+
+
+def collected_by_bits(array, axis):
+    size, index = (lax.axis_size(axis), lax.axis_index(axis))
+    pieces, bit = (array[None], 1)
+    while bit < size:
+        theirs = lax.ppermute(pieces, axis, [(i, i ^ bit) for i in range(size)])
+        low = index & bit == 0
+        pieces = jnp.concatenate([jnp.where(low, pieces, theirs), jnp.where(low, theirs, pieces)])
+        bit *= 2
+    return pieces
+
+
+def collect(x, axis, dim):
+    return joined_along(collected_by_bits(x, axis), dim)
 
 
 def decay_matrix(cumulative):
@@ -110,11 +131,8 @@
         )
         * inverse
     )
-    shard_piece = lax.all_gather(
-        local_back.reshape(1, micro_count, head_count, flat_size).astype(jnp.bfloat16),
-        "seq",
-        axis=0,
-        tiled=True,
+    shard_piece = collect(
+        local_back.reshape(1, micro_count, head_count, flat_size).astype(jnp.bfloat16), "seq", 0
     ).astype(jnp.float32)
     piece_rows = shard_piece.shape[0]
     position = jnp.arange(piece_rows, dtype=jnp.int32)

time: 171 us -> 196 us (1.15)
  waiting for transfers between devices: 47.1 us -> 74.9 us
  blocking collectives: 33 us -> 17.4 us
  matrix products: 37.6 us -> 41.9 us
  other arithmetic: 6 us -> 10.2 us
  starting transfers between devices: 0.3 us -> 4.36 us
    ppermute x0 -> x2, waiting for transfers between devices: none -> 26.2 us  [collected_by_bits(): theirs = lax.ppermute(pieces, axis, [(i, i ^ bit) for i in range(size)])]
    all_gather x1 -> x0, blocking collectives: 15.6 us -> none  [local(): lax.all_gather(local_back.reshape(1, micro_count, head_count, flat_size)....]
    reduce_scatter x1, waiting for transfers between devices: 0.01 us -> 14.2 us  [local(): lax.psum_scatter(reduced, 'dp', scatter_dimension=0, tiled=True)]
    reduce_scatter x1, waiting for transfers between devices: 41.6 us -> 29.6 us  [local(): lax.psum_scatter(reordered.astype(jnp.bfloat16), 'seq', scatter_dimension...]
    ppermute x0 -> x2, starting transfers between devices: none -> 4.02 us  [collected_by_bits(): theirs = lax.ppermute(pieces, axis, [(i, i ^ bit) for i in range(size)])]
    dot_general x1, matrix products: 0.81 us -> 3.66 us  [local(): jnp.einsum('mhts,mshd->mthd', grad_weights, key_heads, preferred_element_...]
    select_n x0 -> x2, other arithmetic: none -> 2.03 us  [collected_by_bits(): jnp.where(low, pieces, theirs)]
    unnamed x25 -> x35, local copies, waits for them, and re-layouts: 9.27 us -> 8.59 us
  transfers between devices with their start and end apart: 3 -> 5, of which waited for: 2 -> 4; matrix products, arithmetic and copies ran while one was open for 33% -> 32% of each run, Pallas kernels for 0% -> 0%
where the time goes in v1:
time: 196 us; the launch traced here: 195 us
  waiting for transfers between devices  74.9 us (38%)
  matrix products  41.9 us (21%)
  local copies, waits for them, and re-layouts  31.7 us (16%)
  blocking collectives  17.4 us (9%)
  between operations  14 us (7%)
  other arithmetic  10.2 us (5%)
  starting transfers between devices  4.36 us (2%)
    reduce_scatter x1, waiting for transfers between devices, local(): lax.psum_scatter(reordered.astype(jnp.bfloat16), 'seq', scatter_dimension...  29.6 us
    ppermute x2, waiting for transfers between devices, collected_by_bits(): theirs = lax.ppermute(pieces, axis, [(i, i ^ bit) for i in range(size)])  26.2 us
    all_gather x1, blocking collectives, local(): lax.all_gather(local_state.reshape(1, micro_count, head_count, flat_size)...  17.4 us
    reduce_scatter x1, waiting for transfers between devices, local(): lax.psum_scatter(reduced, 'dp', scatter_dimension=0, tiled=True)  14.2 us
    another operation x9, local copies, waits for them, and re-layouts  9.03 us
    unnamed x35, local copies, waits for them, and re-layouts  8.59 us
    dot_general x1, matrix products, local(): jnp.einsum('mcd,mcf->df', shard_piece, attn_out, preferred_element_type=j...  5.69 us
    optimization_barrier x1, local copies, waits for them, and re-layouts, local(): lax.optimization_barrier((column_block * grad_scale).astype(jnp.bfloat16))  4.66 us
  transfers between devices with their start and end apart: 5, of which 4 were waited for; matrix products, arithmetic and copies ran while one was open for 32% of the time, Pallas kernels for 0%

profile of v1, /device:TPU:0, one launch (start us, length us, event | category | flops | bytes accessed | tf_op | source)
XLA Modules:
  0.0 194.5 jit_solution(16194467669418107654)
XLA Ops:
  21.1 2.6 %convolution_convert_fusion = bf16[4,128,128]{2,1,0:T(8,128)(2,1)S(1)} fusion(f32[512,4]{0,1:T(4,128)S(1)} %copy.96, bf16[512,4,128]{2,1,0:T(4,128)(2,1)} %reshape.428, bf16[512,4,128]{2,1,0:T(4,128)(2,1)} %reshape.422), kind=kOutput, calls=%fused_computation.24 | convolution fusion | flops 403243008 | bytes 1187840 | tf_op jit(solution)/shard_map/mshd,mshe->mhde/dot_general | solution.py:72
  24.0 17.4 %all_gather.7 = bf16[4,1,4,16384]{3,2,1,0:T(4,128)(2,1)S(1)} all-gather(bf16[1,1,4,16384]{3,2,1,0:T(4,128)(2,1)S(1)} %convert_element_type.129), channel_id=1, replica_groups=mesh['dp'=4,'seq'=4,'tensor'=2] {'seq'}, dimensions={0}, use_global_device_ids=true | all-gather | bytes 655360 | tf_op jit(solution)/shard_map/all_gather | solution.py:75
  45.7 2.8 %multiply_convert_fusion.1 = bf16[4,512,512]{2,1,0:T(8,128)(2,1)S(1)} fusion(f32[4,512]{1,0:T(4,128)S(1)} %bitcast_add_fusion.1, pred[512,512]{1,0:T(8,128)(4,1)S(1)} %iota_compare_fusion, bf16[512,4,128]{2,1,0:T(4,128)(2,1)} %reshape.435, bf16[512,4,128]{2,1,0:T(4,128)(2,1)} %reshape.428), kind=kOutput, calls=%fused_computation.1 | convolution fusion | flops 274726912 | bytes 3416064 | tf_op jit(solution)/shard_map/mthd,mshd->mhts/dot_general | solution.py:68
  50.9 2.2 %fusion.12 = bf16[4,128,512]{2,1,0:T(8,128)(2,1)} fusion(f32[4,128,512]{2,1,0:T(8,128)S(1)} %convolution_bitcast_fusion.1, f32[512,4]{0,1:T(4,128)S(1)} %copy.100, bf16[512,4,128]{2,1,0:T(4,128)(2,1)S(1)} %copy-done.6, f32[1,4,128,128]{3,1,2,0:T(4,128)S(1)} %bitcast.123), kind=kOutput, calls=%fused_computation.21 | convolution fusion | flops 403963904 | bytes 2367488 | tf_op jit(solution)/shard_map/mthd,mhde->mthe/dot_general | solution.py:95
  53.1 4.1 %all-gather.2.cloned.1.call-done = bf16[1,512,3072]{2,1,0:T(8,128)(2,1)} async-done(((bf16[1,512,1536]{2,1,0:T(8,128)(2,1)}), bf16[1,512,3072]{2,1,0:T(8,128)(2,1)}) %all-gather.2.cloned.1.call-update) | async-done | bytes 3145744 | tf_op jit(solution)/shard_map/all_gather | solution.py:103
  57.2 3.8 %fusion.6 = bf16[512,512]{0,1:T(8,128)(2,1)S(1)} fusion(bf16[512,3072]{1,0:T(8,128)(2,1)S(1)} %copy-done, bf16[1,512,3072]{2,1,0:T(8,128)(2,1)} %all-gather.2.cloned.1.call-done), kind=kOutput, calls=%fused_computation.17 | convolution fusion | flops 1610874880 | bytes 6815744 | tf_op jit(solution)/shard_map/mcd,fd->mcf/dot_general | solution.py:104
  61.8 2.8 %multiply_convert_fusion.2 = bf16[4,512,512]{2,1,0:T(8,128)(2,1)} fusion(bf16[512,4,128]{0,2,1:T(8,128)(2,1)S(1)} %bitcast.127, f32[4,512]{1,0:T(4,128)S(1)} %bitcast_add_fusion.1, pred[512,512]{1,0:T(8,128)(4,1)S(1)} %copy-done.14, bf16[512,4,128]{2,1,0:T(4,128)(2,1)S(1)} %copy-done.4), kind=kOutput, calls=%fused_computation.2 | convolution fusion | flops 274726912 | bytes 3416064 | tf_op jit(solution)/shard_map/mthd,mshd->mhts/dot_general | solution.py:124
  64.7 2.0 %copy.99 = bf16[512,4,128]{2,0,1:T(8,128)(2,1)} copy(bf16[512,4,128]{0,2,1:T(8,128)(2,1)} %bitcast.128) | data formatting | bytes 1048576 | tf_op jit(solution)/shard_map/reshape.5
  66.7 3.7 %convolution_bitcast_fusion.2 = f32[4,128,512]{2,1,0:T(8,128)} fusion(bf16[4,512,512]{2,1,0:T(8,128)(2,1)} %multiply_convert_fusion.2, bf16[512,4,128]{2,1,0:T(4,128)(2,1)} %reshape.428), kind=kOutput, calls=%fused_computation.10 | convolution fusion | flops 268435456 | bytes 3670016 | tf_op jit(solution)/shard_map/mhts,mshd->mthd/dot_general | solution.py:149
  71.9 2.0 %fusion.13 = bf16[4,128,128]{2,1,0:T(8,128)(2,1)} fusion(bf16[512,4,128]{0,2,1:T(8,128)(2,1)S(1)} %bitcast.130, f32[512,4]{0,1:T(4,128)S(1)} %copy.100, bf16[512,4,128]{2,1,0:T(4,128)(2,1)S(1)} %copy-done.7), kind=kOutput, calls=%fused_computation.23 | convolution fusion | flops 403308544 | bytes 1187840 | tf_op jit(solution)/shard_map/mthd,mthe->mhde/dot_general | solution.py:129
  76.4 5.7 %fusion = bf16[3072,512]{0,1:T(8,128)(2,1)} fusion(bf16[512,512]{0,1:T(8,128)(2,1)} %bitcast.136, bf16[1,512,3072]{2,1,0:T(8,128)(2,1)} %all-gather.2.cloned.1.call-done), kind=kOutput, calls=%fused_computation.4 | convolution fusion | flops 1613758464 | bytes 6815744 | tf_op jit(solution)/shard_map/mcd,mcf->df/dot_general | solution.py:105
  82.1 2.1 %fusion.9 = bf16[4,128,512]{2,1,0:T(8,128)(2,1)} fusion(f32[4,128,512]{2,1,0:T(8,128)S(1)} %copy-done.9, bf16[512,4,128]{2,0,1:T(8,128)(2,1)S(1)} %copy-done.12, f32[512,4]{0,1:T(4,128)S(1)} %copy.100, f32[1,4,128,128]{3,1,2,0:T(4,128)S(1)} %bitcast.124), kind=kOutput, calls=%fused_computation.18 | convolution fusion | flops 403963904 | bytes 2367488 | tf_op jit(solution)/shard_map/mthe,mhde->mthd/dot_general | solution.py:150
  84.2 2.0 %copy.113 = bf16[1,512,512]{2,1,0:T(8,128)(2,1)} copy(bf16[1,512,512]{1,2,0:T(8,128)(2,1)} %bitcast.131) | data formatting | bytes 1048576
  86.2 4.7 %copy.111 = bf16[3072,512]{1,0:T(8,128)(2,1)} copy(bf16[3072,512]{0,1:T(8,128)(2,1)} %fusion) | data formatting | bytes 6291456 | tf_op jit(solution)/shard_map/optimization_barrier | solution.py:109
  90.9 3.9 %copy.112 = bf16[4,4,192,512]{3,2,1,0:T(8,128)(2,1)} copy(bf16[4,4,192,512]{3,2,0,1:T(8,128)(2,1)} %bitcast.122) | data formatting | bytes 6291456 | tf_op jit(solution)/shard_map/convert_element_type | solution.py:119
  96.3 2.5 %collective-permute-start.1 = (bf16[2,1,1,4,16384]{4,3,2,1,0:T(4,128)(2,1)S(1)}, bf16[2,1,1,4,16384]{4,3,2,1,0:T(4,128)(2,1)S(1)}, u32[]{:S(2)}, u32[]{:S(2)}) collective-permute-start(bf16[2,1,1,4,16384]{4,3,2,1,0:T(4,128)(2,1)S(1)} %pad_maximum_fusion), channel_id=1, source_target_pairs={{0,4},{2,6},{4,0},{6,2},{1,5},{3,7},{5,1},{7,3},{8,12},{10,14},{12... | collective-permute-start | bytes 786440 | tf_op jit(solution)/shard_map/ppermute | solution.py:21
  98.8 3.7 %fusion.55 = f32[4,128,512]{2,1,0:T(8,128)} fusion(bf16[512,4,128]{0,2,1:T(8,128)(2,1)} %bitcast.129, bf16[4,512,512]{2,1,0:T(8,128)(2,1)} %copy-done.1), kind=kOutput, calls=%fused_computation.92 | convolution fusion | flops 268435456 | bytes 3670016 | tf_op jit(solution)/shard_map/mhts,mthd->mshd/dot_general | solution.py:158
  102.5 26.2 %collective-permute-done.1 = bf16[2,1,1,4,16384]{4,3,2,1,0:T(4,128)(2,1)S(1)} collective-permute-done((bf16[2,1,1,4,16384]{4,3,2,1,0:T(4,128)(2,1)S(1)}, bf16[2,1,1,4,16384]{4,3,2,1,0:T(4,128)(2,1)S(1)}, u32[]{:S(2)}, u32[]{:S(2)}) %collective-permute-start.1) | collective-permute-done | bytes 262176 | tf_op jit(solution)/shard_map/ppermute | solution.py:21
  129.7 29.6 %reduce-scatter.3.cloned.1.call-done = bf16[768,512]{1,0:T(8,128)(2,1)} async-done(((bf16[3072,512]{1,0:T(8,128)(2,1)}), bf16[768,512]{1,0:T(8,128)(2,1)}) %reduce-scatter.3.cloned.1.call-update) | async-done | bytes 786448 | tf_op jit(solution)/shard_map/reduce_scatter | solution.py:118
  162.4 2.1 %fusion.10 = bf16[4,128,512]{2,1,0:T(8,128)(2,1)} fusion(f32[4,128,512]{2,1,0:T(8,128)S(1)} %copy-done.8, f32[512,4]{0,1:T(4,128)S(1)} %copy.96, bf16[512,4,128]{2,1,0:T(4,128)(2,1)S(1)} %copy-done.5, f32[1,4,128,128]{3,1,2,0:T(4,128)S(1)} %bitcast.125), kind=kOutput, calls=%fused_computation.19 | convolution fusion | flops 403701760 | bytes 2367488 | tf_op jit(solution)/shard_map/mshe,mhde->mshd/dot_general | solution.py:157
  164.4 2.0 %copy.114 = bf16[1,512,512]{2,1,0:T(8,128)(2,1)} copy(bf16[1,512,512]{1,2,0:T(8,128)(2,1)} %bitcast.133) | data formatting | bytes 1048576
  166.5 3.6 %fusion.11 = bf16[4,128,512]{2,1,0:T(8,128)(2,1)} fusion(f32[4,128,512]{2,1,0:T(8,128)} %fusion.55, f32[512,4]{0,1:T(4,128)S(1)} %copy.96, bf16[512,4,128]{2,1,0:T(4,128)(2,1)} %reshape.428, f32[1,4,128,128]{3,1,2,0:T(4,128)S(1)} %bitcast.126), kind=kOutput, calls=%fused_computation.20 | convolution fusion | flops 403701760 | bytes 2367488 | tf_op jit(solution)/shard_map/mshd,mhde->mshe/dot_general | solution.py:160
  170.0 2.1 %copy.115 = bf16[1,512,512]{2,1,0:T(8,128)(2,1)} copy(bf16[1,512,512]{1,2,0:T(8,128)(2,1)} %bitcast.132) | data formatting | bytes 1048576
  172.1 14.2 %reduce-scatter.5.cloned.1.call-done = bf16[192,512]{1,0:T(8,128)(2,1)} async-done(((bf16[768,512]{1,0:T(8,128)(2,1)}), bf16[192,512]{1,0:T(8,128)(2,1)}) %reduce-scatter.5.cloned.1.call-update) | async-done | bytes 196624 | tf_op jit(solution)/shard_map/reduce_scatter | solution.py:121
  (80 shorter events, 32.8 us)
Async XLA Ops:
  7.2 50.1 %copy-start = (bf16[512,3072]{1,0:T(8,128)(2,1)S(1)}, bf16[512,3072]{1,0:T(8,128)(2,1)}, u32[]{:S(2)}) copy-start(bf16[512,3072]{1,0:T(8,128)(2,1)} %param.10) | copy-start | bytes 9437188
  7.2 50.1 %all-gather.2.cloned.1.call-start = ((), (), s32[]{:S(2)}) async-start(), calls=%async_computation.2 | async-start | bytes 4718592 | tf_op jit(solution)/shard_map/all_gather | solution.py:103
  7.9 151.4 %reduce-scatter.3.cloned.1.call-start = ((), (), s32[]{:S(2)}) async-start(), calls=%async_computation.3 | async-start | bytes 3932160 | tf_op jit(solution)/shard_map/reduce_scatter | solution.py:118
  45.7 2.8 %copy-start.13 = (pred[512,512]{1,0:T(8,128)(4,1)}, pred[512,512]{1,0:T(8,128)(4,1)S(1)}, u32[]{:S(2)}) copy-start(pred[512,512]{1,0:T(8,128)(4,1)S(1)} %iota_compare_fusion) | copy-start | bytes 786436
  45.7 4.2 %copy-start.3 = (bf16[512,4,128]{2,1,0:T(4,128)(2,1)S(1)}, bf16[512,4,128]{2,1,0:T(4,128)(2,1)}, u32[]{:S(2)}) copy-start(bf16[512,4,128]{2,1,0:T(4,128)(2,1)} %reshape.422) | copy-start | bytes 1572868
  48.5 1.4 copy-start.1
  49.9 1.0 copy-start.6
  57.2 4.6 %copy-start.4 = (bf16[512,4,128]{2,1,0:T(4,128)(2,1)S(1)}, bf16[512,4,128]{2,1,0:T(4,128)(2,1)}, u32[]{:S(2)}) copy-start(bf16[512,4,128]{2,1,0:T(4,128)(2,1)} %reshape.422) | copy-start | bytes 1572868
  57.2 4.6 %copy-start.14 = (pred[512,512]{1,0:T(8,128)(4,1)S(1)}, pred[512,512]{1,0:T(8,128)(4,1)}, u32[]{:S(2)}) copy-start(pred[512,512]{1,0:T(8,128)(4,1)} %copy-done.13) | copy-start | bytes 786436
  61.0 0.8 copy-start.10
  66.7 3.7 %copy-start.2 = (bf16[4,512,512]{2,1,0:T(8,128)(2,1)S(1)}, bf16[4,512,512]{2,1,0:T(8,128)(2,1)}, u32[]{:S(2)}) copy-start(bf16[4,512,512]{2,1,0:T(8,128)(2,1)} %multiply_convert_fusion.2) | copy-start | bytes 6291460
  66.7 3.7 %copy-start.7 = (bf16[512,4,128]{2,1,0:T(4,128)(2,1)S(1)}, bf16[512,4,128]{2,1,0:T(4,128)(2,1)}, u32[]{:S(2)}) copy-start(bf16[512,4,128]{2,1,0:T(4,128)(2,1)} %reshape.435) | copy-start | bytes 1572868
  66.7 5.1 %copy-start.11 = (bf16[512,512]{0,1:T(8,128)(2,1)S(1)}, bf16[512,512]{0,1:T(8,128)(2,1)}, u32[]{:S(2)}) copy-start(bf16[512,512]{0,1:T(8,128)(2,1)} %copy-done.10) | copy-start | bytes 1572868
  74.8 20.2 %collective-permute-start = (bf16[1,1,1,4,16384]{4,3,2,1,0:T(4,128)(2,1)S(1)}, bf16[1,1,1,4,16384]{4,3,2,1,0:T(4,128)(2,1)}, u32[]{:S(2)}, u32[]{:S(2)}) collective-permute-start(bf16[1,1,1,4,16384]{4,3,2,1,0:T(4,128)(2,1)S(1)} %convert_element_type.136), channel_id=1, source_target_pairs={{0,2},{2,0},{4,6},{6,4},{1,3},{3,1},{5,7},{7,5},{8,10},{10,8},{12,... | collective-permute-start | bytes 393224 | tf_op jit(solution)/shard_map/ppermute | solution.py:21
  76.4 5.7 %copy-start.9 = (f32[4,128,512]{2,1,0:T(8,128)S(1)}, f32[4,128,512]{2,1,0:T(8,128)}, u32[]{:S(2)}) copy-start(f32[4,128,512]{2,1,0:T(8,128)} %convolution_bitcast_fusion.2) | copy-start | bytes 3145732
  76.4 5.7 %copy-start.12 = (bf16[512,4,128]{2,0,1:T(8,128)(2,1)S(1)}, bf16[512,4,128]{2,0,1:T(8,128)(2,1)}, u32[]{:S(2)}) copy-start(bf16[512,4,128]{2,0,1:T(8,128)(2,1)} %copy.99) | copy-start | bytes 1572868
  94.8 91.5 %reduce-scatter.5.cloned.1.call-start = ((), (), s32[]{:S(2)}) async-start(), calls=%async_computation.4 | async-start | bytes 983040 | tf_op jit(solution)/shard_map/reduce_scatter | solution.py:121
  96.3 64.5 %copy-start.15 = (f32[4,4]{1,0:T(4,128)S(1)}, f32[4,4]{1,0:T(4,128)}, u32[]{:S(2)}) copy-start(f32[4,4]{1,0:T(4,128)} %get-tuple-element.26) | copy-start | bytes 196
  96.3 32.4 %collective-permute-start.1 = (bf16[2,1,1,4,16384]{4,3,2,1,0:T(4,128)(2,1)S(1)}, bf16[2,1,1,4,16384]{4,3,2,1,0:T(4,128)(2,1)S(1)}, u32[]{:S(2)}, u32[]{:S(2)}) collective-permute-start(bf16[2,1,1,4,16384]{4,3,2,1,0:T(4,128)(2,1)S(1)} %pad_maximum_fusion), channel_id=1, source_target_pairs={{0,4},{2,6},{4,0},{6,2},{1,5},{3,7},{5,1},{7,3},{8,12},{10,14},{12... | collective-permute-start | bytes 786440 | tf_op jit(solution)/shard_map/ppermute | solution.py:21
  159.4 3.0 %copy-start.5 = (bf16[512,4,128]{2,1,0:T(4,128)(2,1)S(1)}, bf16[512,4,128]{2,1,0:T(4,128)(2,1)}, u32[]{:S(2)}) copy-start(bf16[512,4,128]{2,1,0:T(4,128)(2,1)} %reshape.422) | copy-start | bytes 1572868
  159.4 3.0 %copy-start.8 = (f32[4,128,512]{2,1,0:T(8,128)S(1)}, f32[4,128,512]{2,1,0:T(8,128)}, u32[]{:S(2)}) copy-start(f32[4,128,512]{2,1,0:T(8,128)} %convolution_bitcast_fusion) | copy-start | bytes 3145732
Sparse Core Ops, SparseCore 0:
  9.5 47.6 all-gather.1
  94.9 64.3 reduce-scatter.2
  161.9 24.3 reduce-scatter.4
